TPU v7x, 32 devices: a whole 2x2x4 slice. The times are simulated.
32 devices in a mesh: vocab: 8 (over y, x, core), hid: 4 (over z).
Axes of the slice: x: 2, y: 2, z: 4, core: 2. Of those that a mesh axis runs over, the one named last changes fastest.
Arguments:
- hidden: bfloat16 [1, 1024, 3584], P(None, 'vocab', 'hid'), may hold values from -30 to 30
- unembed: bfloat16 [3584, 81920], P(None, ('vocab', 'hid')), may hold values from -10 to 10
- labels: int32 [1024], P('vocab'), may hold values from 0 to 81919
Outputs:
- token_loss: float32 [1, 1024], replicated
- layer_loss: float32 [1], replicated
All inputs are finite; a program needn't handle non-finite values.
Results may differ from a plain program's by a relative error of at most 0.0003.
Values may be sent and summed in bfloat16 or wider, within the bound.
A program may use at most 128 MiB of HBM per device.

v0:
```python
import jax
import jax.numpy as jnp
from jax import lax
from jax.sharding import PartitionSpec as P


def block_stats(logits, wanted, first_col):
    row_peak = jnp.max(logits, axis=-1)
    row_total = jnp.sum(jnp.exp(logits - row_peak[..., None]), axis=-1)
    columns = first_col + lax.broadcasted_iota(jnp.int32, (1, 1, logits.shape[-1]), 2)
    picked = jnp.sum(jnp.where(wanted[..., None] == columns, logits, 0.0), axis=-1)
    return (row_peak, row_total, picked)


def fold_tokens(layers, weights, first_col):
    vocab_cols = weights.shape[1]

    def add_tokens(held_stats, pieces, offset):
        piece_rows, wanted = pieces
        row_count = piece_rows.shape[1]
        logits = jnp.dot(
            piece_rows.reshape(-1, piece_rows.shape[2]), weights, preferred_element_type=jnp.float32
        )
        part_stats = block_stats(logits.reshape(layers, row_count, vocab_cols), wanted, first_col)
        return tuple((new_value for new_value in part_stats))

    return add_tokens


def body(hidden, unembed, labels):
    layers = hidden.shape[0]
    vocab_cols = unembed.shape[1]
    first_col = lax.axis_index(("vocab", "hid")) * vocab_cols
    targets = labels.reshape(1, -1)
    tokens_all = labels.shape[0] * lax.axis_size("vocab")
    full_rows = lax.all_gather(hidden, "hid", axis=2, tiled=True)
    add_tokens = fold_tokens(layers, unembed, first_col)
    blank_stats = jnp.zeros((layers, tokens_all), jnp.float32)
    row_peak, row_total, picked = add_tokens(
        (blank_stats, blank_stats, blank_stats),
        (
            lax.all_gather(full_rows, "vocab", axis=1, tiled=True),
            lax.all_gather(targets, "vocab", axis=1, tiled=True),
        ),
        jnp.int32(0),
    )
    highest = lax.pmax(row_peak, ("vocab", "hid"))
    row_total, picked = lax.psum(
        (row_total * jnp.exp(row_peak - highest), picked), ("vocab", "hid")
    )
    row_peak = highest
    token_loss = row_peak + jnp.log(row_total) - picked
    return (token_loss, jnp.mean(token_loss, axis=1))


def solution(mesh):
    placed = (P(None, "vocab", "hid"), P(None, ("vocab", "hid")), P("vocab"))
    return jax.shard_map(body, mesh=mesh, in_specs=placed, out_specs=(P(), P()), check_vma=False)
```

profile of v0, /device:TPU:0, one launch (start us, length us, event | category | flops | bytes accessed | tf_op | source)
XLA Modules:
  0.0 201.6 jit_solution(13099708919454776192)
XLA Ops:
  7.2 0.0 all-gather.4.cloned.1.call-start
  7.2 23.5 %all_gather.9 = bf16[1,128,3584]{2,1,0:T(8,128)(2,1)} all-gather(bf16[1,128,896]{2,1,0:T(8,128)(2,1)} %param.3), channel_id=1, replica_groups=mesh['vocab'=8,'hid'=4] {'hid'}, dimensions={2}, use_global_device_ids=true | all-gather | bytes 1146880 | tf_op jit(solution)/shard_map/all_gather | solution.py:36
  30.7 0.0 all-gather.4.cloned.1.call-update
  30.8 8.9 %all-gather.1 = s32[8,1,128]{2,1,0:T(1,128)S(1)} all-gather(s32[1,1,128]{2,1,0:T(1,128)} %bitcast.17), channel_id=2, replica_groups=mesh['vocab'=8,'hid'=4] {'vocab'}, dimensions={0}, use_global_device_ids=true | all-gather | bytes 4608 | tf_op jit(solution)/shard_map/all_gather | solution.py:43
  39.7 40.4 %all-gather.4.cloned.1.call-done = bf16[1,1024,3584]{2,1,0:T(8,128)(2,1)} async-done(((bf16[1,128,3584]{2,1,0:T(8,128)(2,1)}), bf16[1,1024,3584]{2,1,0:T(8,128)(2,1)}) %all-gather.4.cloned.1.call-update) | async-done | bytes 7340048 | tf_op jit(solution)/shard_map/all_gather | solution.py:42
  80.1 25.8 %fusion.3 = (f32[1024]{0:T(1024)S(1)}, f32[1024,2560]{1,0:T(8,128)}) fusion(bf16[3584,2560]{1,0:T(8,128)(2,1)} %param.4, bf16[1,1024,3584]{2,1,0:T(8,128)(2,1)} %all-gather.4.cloned.1.call-done), kind=kOutput, calls=%fused_computation.8 | convolution fusion | flops 18793103360 | bytes 36179968 | tf_op jit(solution)/shard_map/dot_general | solution.py:21
  105.9 39.3 %pmax.7 = f32[1,1024]{1,0:T(1,128)S(1)} all-reduce(f32[1,1024]{1,0:T(1,128)S(1)} %bitcast.12), channel_id=1, replica_groups=mesh['vocab'=8,'hid'=4] {'vocab','hid'}, use_global_device_ids=true, to_apply=%region_1.0 | all-reduce | flops 1024 | bytes 8192 | tf_op jit(solution)/shard_map/pmax | solution.py:47
  145.2 5.5 %exponential_reduce_fusion = (f32[1024]{0:T(1024)S(1)}, f32[1024]{0:T(1024)S(1)}) fusion(f32[1024,2560]{1,0:T(8,128)} %get-tuple-element.9, f32[1024]{0:T(1024)S(1)} %get-tuple-element.8, s32[2560]{0:T(1024)S(1)} %iota_add_fusion, s32[1024]{0:T(1024)S(1)} %bitcast.14), kind=kLoop, calls=%fused_computation.1 | loop fusion | flops 13105152 | bytes 10512384 | tf_op jit(solution)/shard_map/reduce_sum | solution.py:9
  150.7 41.1 %all-reduce = (f32[1,1024]{1,0:T(1,128)S(1)}, f32[1,1024]{1,0:T(1,128)S(1)}) all-reduce(f32[1,1024]{1,0:T(1,128)S(1)} %bitcast.15, f32[1,1024]{1,0:T(1,128)S(1)} %exponential_multiply_fusion), channel_id=1, replica_groups=mesh['vocab'=8,'hid'=4] {'vocab','hid'}, use_global_device_ids=true, to_apply=%region_5.6 | all-reduce | flops 2048 | bytes 16384 | tf_op jit(solution)/shard_map/psum | solution.py:48
  191.7 1.2 fusion.2
  (2 shorter events, 0.0 us)
Async XLA Ops:
  7.2 73.0 %all-gather.4.cloned.1.call-start = ((), (), s32[]{:S(2)}) async-start(), calls=%async_computation | async-start | bytes 8257536 | tf_op jit(solution)/shard_map/all_gather | solution.py:42
Sparse Core Ops, SparseCore 0:
  30.9 49.1 all-gather.3
where the time goes:
time: 202 us
  blocking collectives  113 us (56%)
  waiting for transfers between devices  40.4 us (20%)
  matrix products  25.8 us (13%)
  between operations  15.8 us (8%)
  other arithmetic  6.69 us (3%)
    psum x1, blocking collectives, body(): lax.psum((row_total * jnp.exp(row_peak - highest), picked), ('vocab', 'hi...  41.1 us
    all_gather x1, waiting for transfers between devices, body(): lax.all_gather(full_rows, 'vocab', axis=1, tiled=True)  40.4 us
    pmax x1, blocking collectives, body(): highest = lax.pmax(row_peak, ('vocab', 'hid'))  39.3 us
    dot_general x1, matrix products, add_tokens(): jnp.dot(piece_rows.reshape(-1, piece_rows.shape[2]), weights, preferred_e...  25.8 us
    all_gather x1, blocking collectives, body(): full_rows = lax.all_gather(hidden, 'hid', axis=2, tiled=True)  23.5 us
    all_gather x1, blocking collectives, body(): lax.all_gather(targets, 'vocab', axis=1, tiled=True)  8.92 us
    reduce_sum x1, other arithmetic, block_stats(): row_total = jnp.sum(jnp.exp(logits - row_peak[..., None]), axis=-1)  5.47 us
  transfers between devices with their start and end apart: 1, of which 1 were waited for; matrix products, arithmetic and copies ran while one was open for 0% of the time, Pallas kernels for 0%

commit v1 on v0

v1 whole, which is shorter than its diff:
```python
import functools

import jax
import jax.numpy as jnp
from jax import lax
from jax.experimental import pallas as pl
from jax.experimental.pallas import tpu as pltpu
from jax.sharding import PartitionSpec as P

MESH = pl.DeviceIdType.MESH
LANES = 128


def bits_of(mask):
    return [1 << b for b in range(mask.bit_length()) if mask >> b & 1]


def parent_dim(group, piece):
    dims = bits_of(group)
    return dims[piece % len(dims)]


def flip(index, mask):
    for bit in bits_of(mask):
        index = index + bit - 2 * bit * lax.rem(index // bit, 2)
    return index


def combine(parts, blocks):
    peaks = [part[0:blocks] for part in parts]
    peak = functools.reduce(jnp.maximum, peaks)
    total = sum(part[blocks : 2 * blocks] * jnp.exp(own - peak) for part, own in zip(parts, peaks))
    picked = sum(part[2 * blocks : 3 * blocks] for part in parts)
    return peak, total, picked


def kernel(
    n_v, n_h, layers,
    hid_hbm, w_hbm, lab_ref,
    loss_ref,
    buf, w, acc, labs, part, rel_stats, line, plane,
    own_sem, w_sem, send_sem, recv_sem, lab_send, lab_recv, line_send, line_recv, plane_send, plane_recv,
):
    v, z = lax.axis_index("vocab"), lax.axis_index("hid")
    rows = hid_hbm.shape[0]
    depth = hid_hbm.shape[1]
    cols = w_hbm.shape[1]
    first_col = (v * n_h + z) * cols
    dims = [1 << b for b in range((n_v // 2).bit_length() - 1)]
    groups = sorted(range(n_v // 2), key=lambda g: (len(bits_of(g)), g))
    pos = {2 * g + c: 2 * i + c for i, g in enumerate(groups) for c in range(2)}
    blocks = n_v * layers

    own = pltpu.make_async_copy(hid_hbm, buf.at[0, pl.ds(0, rows)], own_sem)
    own.start()
    w_copies = []
    for s in range(n_h):
        src = lax.rem(z - s + n_h, n_h)
        copy = pltpu.make_async_copy(
            w_hbm.at[pl.ds(pl.multiple_of(src * depth, depth), depth)], w.at[s], w_sem.at[s]
        )
        w_copies.append(copy)

    barrier = pltpu.get_barrier_semaphore()
    line_peers = [lax.rem(z + j, n_h) for j in range(1, n_h)]
    for peer in line_peers:
        pl.semaphore_signal(barrier, inc=1, device_id=(v, peer), device_id_type=MESH)
    for m in range(1, n_v):
        pl.semaphore_signal(barrier, inc=1, device_id=(flip(v, m), z), device_id_type=MESH)
    for copy in w_copies:
        copy.start()
    pl.semaphore_wait(barrier, n_h + n_v - 2)
    own.wait()

    sends = []

    def block_at(m, s):
        return buf.at[s, pl.ds(pos[m] * rows, rows)]

    def block_copy(m, s, to_m, to_s, device):
        k = len(sends)
        return pltpu.make_async_remote_copy(
            src_ref=block_at(m, s), dst_ref=block_at(to_m, to_s),
            send_sem=send_sem.at[min(k, send_sem.shape[0] - 1)],
            recv_sem=recv_sem.at[to_m * n_h + to_s],
            device_id=device, device_id_type=MESH,
        )

    def send(m, s, to_m, to_s, device):
        copy = block_copy(m, s, to_m, to_s, device)
        copy.start()
        sends.append(copy)

    def wait_block(m, s):
        if (m, s) != (0, 0):
            block_copy(m, s, m, s, (flip(v, 1), z)).wait_recv()

    def to_line(s):
        if s < n_h - 1:
            send(0, s, 0, s + 1, (v, lax.rem(z + 1, n_h)))

    def to_dims(g, s):
        for d in dims:
            if not g & d and parent_dim(g | d, s) == d:
                send(2 * g, s, 2 * (g | d), s, (flip(v, 2 * d), z))

    def to_pair(g, s):
        send(2 * g, s, 2 * g + 1, s, (flip(v, 1), z))

    tile = max(t for t in (512, 384, 256, 128) if cols % t == 0)

    def multiply(first, count, s):
        lo, size = first * 2 * rows, count * 2 * rows
        step = 1024 if size > 1024 and size % 1024 == 0 else size

        @pl.loop(0, cols // tile)
        def _(n):
            at = pl.ds(pl.multiple_of(n * tile, tile), tile)
            for r in range(lo, lo + size, step):
                value = jnp.dot(
                    buf[s, r : r + step, :], w[s, :, at], preferred_element_type=jnp.float32
                )
                if s == 0:
                    acc[r : r + step, at] = value
                else:
                    acc[r : r + step, at] = acc[r : r + step, at] + value

    def stats(first, count):
        half = 64

        @pl.loop(first * 2 * layers, (first + count) * 2 * layers)
        def _(p):
            label = labs[p // layers].astype(jnp.float32)
            label = jnp.transpose(jnp.broadcast_to(label, (LANES, LANES)))
            lane = lax.broadcasted_iota(jnp.int32, (half, LANES), 1) + first_col
            lane = lane.astype(jnp.float32)
            for h in range(LANES // half):
                at = pl.ds(pl.multiple_of(p * LANES + h * half, half), half)
                peak = acc[at, 0:LANES]
                for c in range(LANES, cols, LANES):
                    peak = jnp.maximum(peak, acc[at, c : c + LANES])
                here = slice(h * half, (h + 1) * half)
                part[0, here, :] = peak
                row_peak = jnp.max(peak, axis=1, keepdims=True)
                row_peak = jnp.broadcast_to(row_peak, (half, LANES))
                wanted = label[here] - lane
                total = jnp.zeros((half, LANES), jnp.float32)
                picked = jnp.zeros((half, LANES), jnp.float32)
                for c in range(0, cols, LANES):
                    x = acc[at, c : c + LANES]
                    total = total + jnp.exp(x - row_peak)
                    picked = picked + jnp.where(wanted == float(c), x, 0.0)
                part[1, here, :] = total
                part[2, here, :] = picked
            rel_stats[0, p] = jnp.max(jnp.transpose(part[0]), axis=0, keepdims=True)
            rel_stats[1, p] = jnp.sum(jnp.transpose(part[1]), axis=0, keepdims=True)
            rel_stats[2, p] = jnp.sum(jnp.transpose(part[2]), axis=0, keepdims=True)

    to_line(0)
    to_dims(0, 0)
    to_pair(0, 0)
    lab_copies = []
    for m in range(1, n_v):
        copy = pltpu.make_async_remote_copy(
            src_ref=lab_ref, dst_ref=labs.at[pos[m]],
            send_sem=lab_send.at[m - 1], recv_sem=lab_recv.at[m - 1],
            device_id=(flip(v, m), z), device_id_type=MESH,
        )
        copy.start()
        lab_copies.append(copy)
    labs[0] = lab_ref[...]

    near = [g for g in groups if len(bits_of(g)) == 1]
    far = [g for g in groups if len(bits_of(g)) > 1]
    for s in range(1, n_h + 1):
        if s < n_h:
            wait_block(0, s)
            to_line(s)
            to_dims(0, s)
            to_pair(0, s)
        for g in near:
            wait_block(2 * g, s - 1)
            to_pair(g, s - 1)
        late = range(s) if s == n_h - 1 else ([s - 1] if s == n_h else [])
        for t in late:
            for g in near:
                to_dims(g, t)
        for g in [0] + near:
            wait_block(2 * g + 1, s - 1)
        w_copies[s - 1].wait()
        multiply(0, 1 + len(near), s - 1)
    for copy in lab_copies:
        copy.wait()
    if not far:
        stats(0, 1 + len(near))
    else:
        levels = sorted({len(bits_of(g)) for g in far})
        done = 1 + len(near)
        stats(0, done)
        for level in levels:
            here = [g for g in far if len(bits_of(g)) == level]
            for s in range(n_h):
                for g in here:
                    wait_block(2 * g, s)
                    to_dims(g, s)
                    to_pair(g, s)
            for s in range(n_h):
                for g in here:
                    wait_block(2 * g + 1, s)
                multiply(done, len(here), s)
            stats(done, len(here))
            done += len(here)

    for m in range(n_v):
        for l in range(layers):
            for k in range(3):
                line[z, pl.ds(k * blocks + flip(v, m) * layers + l, 1), :] = rel_stats[k, pos[m] * layers + l]
    line_copies = []
    for j, peer in enumerate(line_peers):
        copy = pltpu.make_async_remote_copy(
            src_ref=line.at[z], dst_ref=line.at[z],
            send_sem=line_send.at[j], recv_sem=line_recv.at[j],
            device_id=(v, peer), device_id_type=MESH,
        )
        copy.start()
        line_copies.append(copy)
    for copy in line_copies:
        copy.wait_recv()
    peak, total, picked = combine([line[h] for h in range(n_h)], blocks)
    plane[v, 0:blocks, :] = peak
    plane[v, blocks : 2 * blocks, :] = total
    plane[v, 2 * blocks : 3 * blocks, :] = picked
    plane_copies = []
    for m in range(1, n_v):
        copy = pltpu.make_async_remote_copy(
            src_ref=plane.at[v], dst_ref=plane.at[v],
            send_sem=plane_send.at[m - 1], recv_sem=plane_recv.at[m - 1],
            device_id=(flip(v, m), z), device_id_type=MESH,
        )
        copy.start()
        plane_copies.append(copy)
    for copy in sends + line_copies:
        copy.wait_send()
    for copy in plane_copies:
        copy.wait_recv()
    peak, total, picked = combine([plane[u] for u in range(n_v)], blocks)
    loss_ref[...] = peak + jnp.log(total) - picked
    for copy in plane_copies:
        copy.wait_send()


def body(hidden, unembed, labels, n_v, n_h):
    layers, tokens, depth = hidden.shape
    cols = unembed.shape[1]
    rows = layers * tokens
    blocks = n_v * layers
    dma = pltpu.SemaphoreType.DMA
    any_space = pl.BlockSpec(memory_space=pl.ANY)
    vmem = pl.BlockSpec(memory_space=pltpu.VMEM)
    loss = pl.pallas_call(
        functools.partial(kernel, n_v, n_h, layers),
        out_shape=jax.ShapeDtypeStruct((blocks, tokens), jnp.float32),
        in_specs=[any_space, any_space, vmem],
        out_specs=vmem,
        scratch_shapes=[
            pltpu.VMEM((n_h, n_v * rows, depth), jnp.bfloat16),
            pltpu.VMEM((n_h, depth, cols), jnp.bfloat16),
            pltpu.VMEM((n_v * rows, cols), jnp.float32),
            pltpu.VMEM((n_v, 1, tokens), jnp.int32),
            pltpu.VMEM((3, LANES, LANES), jnp.float32),
            pltpu.VMEM((3, blocks, 1, tokens), jnp.float32),
            pltpu.VMEM((n_h, 3 * blocks, tokens), jnp.float32),
            pltpu.VMEM((n_v, 3 * blocks, tokens), jnp.float32),
            dma,
            dma((n_h,)),
            dma((n_v * n_h - 1,)),
            dma((n_v * n_h,)),
            dma((n_v - 1,)),
            dma((n_v - 1,)),
            dma((n_h - 1,)),
            dma((n_h - 1,)),
            dma((n_v - 1,)),
            dma((n_v - 1,)),
        ],
        compiler_params=pltpu.CompilerParams(
            collective_id=0, has_side_effects=True, vmem_limit_bytes=60 * 2**20
        ),
    )(hidden.reshape(rows, depth), unembed, labels.reshape(1, tokens))
    token_loss = loss.reshape(n_v, layers, tokens).transpose(1, 0, 2).reshape(layers, n_v * tokens)
    return token_loss, jnp.mean(token_loss, axis=1)


def solution(mesh):
    placed = (P(None, "vocab", "hid"), P(None, ("vocab", "hid")), P("vocab"))
    inner = functools.partial(body, n_v=mesh.shape["vocab"], n_h=mesh.shape["hid"])
    return jax.shard_map(inner, mesh=mesh, in_specs=placed, out_specs=(P(), P()), check_vma=False)
```

time: 202 us -> 67.7 us (0.34)
  blocking collectives: 113 us -> 0 us
  Pallas kernels: 0 us -> 62.5 us
  waiting for transfers between devices: 40.4 us -> 0 us
  matrix products: 25.8 us -> 0 us
  between operations: 15.8 us -> 2.42 us
  other arithmetic: 6.69 us -> 1.29 us
    pallas_call x0 -> x1, Pallas kernels: none -> 62.5 us  [body(): pl.pallas_call(functools.partial(kernel, n_v, n_h, layers), out_shape=jax...]
    psum x1 -> x0, blocking collectives: 41.1 us -> none  [body(): lax.psum((row_total * jnp.exp(row_peak - highest), picked), ('vocab', 'hi...]
    all_gather x1 -> x0, waiting for transfers between devices: 40.4 us -> none  [body(): lax.all_gather(full_rows, 'vocab', axis=1, tiled=True)]
    pmax x1 -> x0, blocking collectives: 39.3 us -> none  [body(): highest = lax.pmax(row_peak, ('vocab', 'hid'))]
    all_gather x2 -> x0, blocking collectives: 32.4 us -> none  [the longest x1 23.5 us: body(): full_rows = lax.all_gather(hidden, 'hid', axis=2, tiled=True)]
    dot_general x1 -> x0, matrix products: 25.8 us -> none  [add_tokens(): jnp.dot(piece_rows.reshape(-1, piece_rows.shape[2]), weights, preferred_e...]
    reduce_sum x1 -> x0, other arithmetic: 5.47 us -> none  [block_stats(): row_total = jnp.sum(jnp.exp(logits - row_peak[..., None]), axis=-1)]
  transfers between devices with their start and end apart: 1 -> 0, of which waited for: 1 -> 0; matrix products, arithmetic and copies ran while one was open for 0% -> 0% of each run, Pallas kernels for 0% -> 0%
where the time goes in v1:
time: 67.7 us; the launch traced here: 67.5 us
  Pallas kernels  62.5 us (92%)
  between operations  2.42 us (4%)
  other arithmetic  1.29 us (2%)
  local copies, waits for them, and re-layouts  1.28 us (2%)
    pallas_call x1, Pallas kernels, body(): pl.pallas_call(functools.partial(kernel, n_v, n_h, layers), out_shape=jax...  62.5 us

profile of v1, /device:TPU:0, one launch (start us, length us, event | category | flops | bytes accessed | tf_op | source)
XLA Modules:
  0.0 67.5 jit_solution(8732930735186307867)
XLA Ops:
  0.6 62.5 %shard_map.50 = f32[8,128]{1,0:T(8,128)} custom-call(bf16[128,896]{1,0:T(8,128)(2,1)} %bitcast.4, bf16[3584,2560]{1,0:T(8,128)(2,1)} %w_hbm.1, s32[1,128]{1,0:T(1,128)} %bitcast.6), custom_call_target="tpu_custom_call" | custom-call | tf_op jit(solution)/shard_map/pallas_call | solution.py:260
  63.1 1.3 %reduce_sum.9 = f32[]{:T(128)} reduce(f32[8,128]{1,0:T(8,128)} %shard_map.50, f32[]{:T(128)} %constant.4.clone.1), dimensions={0,1}, to_apply=%region_0.0 | reduce | flops 1023 | bytes 4104 | tf_op jit(solution)/shard_map/reduce_sum | solution.py:290
  65.1 1.3 %copy.6 = f32[1,1024]{1,0:T(1,128)} copy(f32[1,1024]{1,0:T(1,128)} %bitcast.5) | data formatting | bytes 8192

commit v2 on v1

--- a/solution.py
+++ b/solution.py
@@ -9,15 +9,27 @@
 
 MESH = pl.DeviceIdType.MESH
 LANES = 128
+CUTS = 2
 
 
 def bits_of(mask):
     return [1 << b for b in range(mask.bit_length()) if mask >> b & 1]
 
 
-def parent_dim(group, piece):
+def via_dim(group, piece):
     dims = bits_of(group)
-    return dims[piece % len(dims)]
+    return dims[piece] if 1 < len(dims) and piece < len(dims) else dims[0] if len(dims) == 1 else None
+
+
+def arrival(group, s):
+    if group == 0:
+        return s
+    dim = via_dim(group, s)
+    if dim is None:
+        return 1 + arrival(group, s - 1)
+    if group == dim:
+        return s + 1 if s < 2 else s + 2
+    return max(3, 1 + arrival(group ^ dim, s))
 
 
 def flip(index, mask):
@@ -37,7 +49,7 @@
 def kernel(
     n_v, n_h, layers,
     hid_hbm, w_hbm, lab_ref,
-    loss_ref,
+    loss_ref, mean_ref,
     buf, w, acc, labs, part, rel_stats, line, plane,
     own_sem, w_sem, send_sem, recv_sem, lab_send, lab_recv, line_send, line_recv, plane_send, plane_recv,
 ):
@@ -72,48 +84,58 @@
     pl.semaphore_wait(barrier, n_h + n_v - 2)
     own.wait()
 
+    cuts = CUTS if n_v * n_h <= 64 else 1
+    piece = rows // cuts
     sends = []
 
-    def block_at(m, s):
-        return buf.at[s, pl.ds(pos[m] * rows, rows)]
-
-    def block_copy(m, s, to_m, to_s, device):
-        k = len(sends)
+    def block_copy(m, s, to_m, to_s, cut, device):
+        k = min(len(sends), send_sem.shape[0] - 1)
         return pltpu.make_async_remote_copy(
-            src_ref=block_at(m, s), dst_ref=block_at(to_m, to_s),
-            send_sem=send_sem.at[min(k, send_sem.shape[0] - 1)],
-            recv_sem=recv_sem.at[to_m * n_h + to_s],
+            src_ref=buf.at[s, pl.ds(pos[m] * rows + cut * piece, piece)],
+            dst_ref=buf.at[to_s, pl.ds(pos[to_m] * rows + cut * piece, piece)],
+            send_sem=send_sem.at[k],
+            recv_sem=recv_sem.at[(to_m * n_h + to_s) * cuts + cut],
             device_id=device, device_id_type=MESH,
         )
 
-    def send(m, s, to_m, to_s, device):
-        copy = block_copy(m, s, to_m, to_s, device)
+    def send(m, s, to_m, to_s, cut, device):
+        copy = block_copy(m, s, to_m, to_s, cut, device)
         copy.start()
         sends.append(copy)
 
-    def wait_block(m, s):
+    def wait_block(m, s, cut):
         if (m, s) != (0, 0):
-            block_copy(m, s, m, s, (flip(v, 1), z)).wait_recv()
-
-    def to_line(s):
-        if s < n_h - 1:
-            send(0, s, 0, s + 1, (v, lax.rem(z + 1, n_h)))
-
-    def to_dims(g, s):
+            block_copy(m, s, m, s, cut, (flip(v, 1), z)).wait_recv()
+
+    def arrive(g, s, cut):
+        wait_block(2 * g, s, cut)
+        if s + 1 < n_h and (g == 0 or via_dim(g, s + 1) is None):
+            send(2 * g, s, 2 * g, s + 1, cut, (v, lax.rem(z + 1, n_h)))
         for d in dims:
-            if not g & d and parent_dim(g | d, s) == d:
-                send(2 * g, s, 2 * (g | d), s, (flip(v, 2 * d), z))
-
-    def to_pair(g, s):
-        send(2 * g, s, 2 * g + 1, s, (flip(v, 1), z))
+            if not g & d and via_dim(g | d, s) == d:
+                send(2 * g, s, 2 * (g | d), s, cut, (flip(v, 2 * d), z))
+        send(2 * g, s, 2 * g + 1, s, cut, (flip(v, 1), z))
 
     tile = max(t for t in (512, 384, 256, 128) if cols % t == 0)
 
-    def multiply(first, count, s):
+    tiles = cols // tile
+    waited = set()
+
+    def multiply(first, count, s, tile_lo, tile_hi):
+        if tile_lo == tile_hi:
+            return
+        for g in groups[first : first + count]:
+            for cut in range(cuts):
+                if (g, s, cut) not in waited:
+                    wait_block(2 * g + 1, s, cut)
+                    waited.add((g, s, cut))
+        if s not in waited:
+            w_copies[s].wait()
+            waited.add(s)
         lo, size = first * 2 * rows, count * 2 * rows
         step = 1024 if size > 1024 and size % 1024 == 0 else size
 
-        @pl.loop(0, cols // tile)
+        @pl.loop(tile_lo, tile_hi)
         def _(n):
             at = pl.ds(pl.multiple_of(n * tile, tile), tile)
             for r in range(lo, lo + size, step):
@@ -156,9 +178,8 @@
             rel_stats[1, p] = jnp.sum(jnp.transpose(part[1]), axis=0, keepdims=True)
             rel_stats[2, p] = jnp.sum(jnp.transpose(part[2]), axis=0, keepdims=True)
 
-    to_line(0)
-    to_dims(0, 0)
-    to_pair(0, 0)
+    for cut in range(cuts):
+        arrive(0, 0, cut)
     lab_copies = []
     for m in range(1, n_v):
         copy = pltpu.make_async_remote_copy(
@@ -170,46 +191,46 @@
         lab_copies.append(copy)
     labs[0] = lab_ref[...]
 
-    near = [g for g in groups if len(bits_of(g)) == 1]
-    far = [g for g in groups if len(bits_of(g)) > 1]
-    for s in range(1, n_h + 1):
-        if s < n_h:
-            wait_block(0, s)
-            to_line(s)
-            to_dims(0, s)
-            to_pair(0, s)
-        for g in near:
-            wait_block(2 * g, s - 1)
-            to_pair(g, s - 1)
-        late = range(s) if s == n_h - 1 else ([s - 1] if s == n_h else [])
-        for t in late:
-            for g in near:
-                to_dims(g, t)
-        for g in [0] + near:
-            wait_block(2 * g + 1, s - 1)
-        w_copies[s - 1].wait()
-        multiply(0, 1 + len(near), s - 1)
+    all_blocks = [(g, s) for s in range(n_h) for g in groups]
+    last = max(arrival(g, s) for g, s in all_blocks)
+    events, jobs = {}, {}
+    for t in range(last + 1):
+        here = [block for block in all_blocks if arrival(*block) == t]
+        events[t] = sorted(here, key=lambda block: (block[0] == 0) == (t == 2))
+        ready = [(g, s) for g, s in all_blocks if t == (s + (s > 0) if g == 0 else arrival(g, s))]
+        jobs[t] = []
+        for g, s in ready:
+            i = groups.index(g)
+            if jobs[t] and jobs[t][-1][2] == s and sum(jobs[t][-1][:2]) == i:
+                first, count, _ = jobs[t].pop()
+                jobs[t].append((first, count + 1, s))
+            else:
+                jobs[t].append((i, 1, s))
+
+    def run(t, lo, hi):
+        total = sum(count for _, count, _ in jobs[t]) * tiles
+        begin, end, at = total * lo // 3, total * hi // 3, 0
+        for first, count, s in jobs[t]:
+            first_tile = min(max(0, (begin - at) // count), tiles)
+            last_tile = min(max(0, (end - at) // count), tiles)
+            multiply(first, count, s, first_tile, last_tile)
+            at += count * tiles
+
+    for t in range(last + 1):
+        for cut in range(cuts):
+            if t > 0:
+                for g, s in events[t]:
+                    arrive(g, s, cut)
+            if t > 1 and cut < cuts - 1:
+                run(t - 1, 1, 2)
+        if t > 1:
+            run(t - 1, 1 if cuts == 1 else 2, 3)
+        run(t, 0, 3 if t == 0 or t == last else 1)
+        if t == 1 and last == 1:
+            run(1, 1, 3)
     for copy in lab_copies:
         copy.wait()
-    if not far:
-        stats(0, 1 + len(near))
-    else:
-        levels = sorted({len(bits_of(g)) for g in far})
-        done = 1 + len(near)
-        stats(0, done)
-        for level in levels:
-            here = [g for g in far if len(bits_of(g)) == level]
-            for s in range(n_h):
-                for g in here:
-                    wait_block(2 * g, s)
-                    to_dims(g, s)
-                    to_pair(g, s)
-            for s in range(n_h):
-                for g in here:
-                    wait_block(2 * g + 1, s)
-                multiply(done, len(here), s)
-            stats(done, len(here))
-            done += len(here)
+    stats(0, len(groups))
 
     for m in range(n_v):
         for l in range(layers):
@@ -244,7 +265,14 @@
     for copy in plane_copies:
         copy.wait_recv()
     peak, total, picked = combine([plane[u] for u in range(n_v)], blocks)
-    loss_ref[...] = peak + jnp.log(total) - picked
+    loss = peak + jnp.log(total) - picked
+    for l in range(layers):
+        sums = jnp.zeros((1, LANES), jnp.float32)
+        for u in range(n_v):
+            row = loss[u * layers + l : u * layers + l + 1]
+            loss_ref[l : l + 1, u * LANES : (u + 1) * LANES] = row
+            sums = sums + row
+        mean_ref[l] = jnp.sum(sums) / (n_v * LANES)
     for copy in plane_copies:
         copy.wait_send()
 
@@ -257,11 +285,15 @@
     dma = pltpu.SemaphoreType.DMA
     any_space = pl.BlockSpec(memory_space=pl.ANY)
     vmem = pl.BlockSpec(memory_space=pltpu.VMEM)
-    loss = pl.pallas_call(
+    cuts = CUTS if n_v * n_h <= 64 else 1
+    return pl.pallas_call(
         functools.partial(kernel, n_v, n_h, layers),
-        out_shape=jax.ShapeDtypeStruct((blocks, tokens), jnp.float32),
+        out_shape=(
+            jax.ShapeDtypeStruct((layers, n_v * tokens), jnp.float32),
+            jax.ShapeDtypeStruct((layers,), jnp.float32),
+        ),
         in_specs=[any_space, any_space, vmem],
-        out_specs=vmem,
+        out_specs=(vmem, pl.BlockSpec(memory_space=pltpu.SMEM)),
         scratch_shapes=[
             pltpu.VMEM((n_h, n_v * rows, depth), jnp.bfloat16),
             pltpu.VMEM((n_h, depth, cols), jnp.bfloat16),
@@ -273,8 +305,8 @@
             pltpu.VMEM((n_v, 3 * blocks, tokens), jnp.float32),
             dma,
             dma((n_h,)),
-            dma((n_v * n_h - 1,)),
-            dma((n_v * n_h,)),
+            dma(((n_v * n_h - 1) * cuts,)),
+            dma((n_v * n_h * cuts,)),
             dma((n_v - 1,)),
             dma((n_v - 1,)),
             dma((n_h - 1,)),
@@ -286,8 +318,6 @@
             collective_id=0, has_side_effects=True, vmem_limit_bytes=60 * 2**20
         ),
     )(hidden.reshape(rows, depth), unembed, labels.reshape(1, tokens))
-    token_loss = loss.reshape(n_v, layers, tokens).transpose(1, 0, 2).reshape(layers, n_v * tokens)
-    return token_loss, jnp.mean(token_loss, axis=1)
 
 
 def solution(mesh):

time: 67.7 us -> 63.7 us (0.941)
  Pallas kernels: 62.5 us -> 59.8 us
  other arithmetic: 1.29 us -> 0 us
    pallas_call x1, Pallas kernels: 62.5 us -> 59.8 us  [body(): pl.pallas_call(functools.partial(kernel, n_v, n_h, layers), out_shape=(ja...]
    reduce_sum x1 -> x0, other arithmetic: 1.29 us -> none  [body(): return (token_loss, jnp.mean(token_loss, axis=1))]
where the time goes in v2:
time: 63.7 us; the launch traced here: 63.5 us
  Pallas kernels  59.8 us (94%)
  between operations  2.4 us (4%)
  local copies, waits for them, and re-layouts  1.26 us (2%)
    pallas_call x1, Pallas kernels, body(): pl.pallas_call(functools.partial(kernel, n_v, n_h, layers), out_shape=(ja...  59.8 us

profile of v2, /device:TPU:0, one launch (start us, length us, event | category | flops | bytes accessed | tf_op | source)
XLA Modules:
  0.0 63.5 jit_solution(1409539765937599370)
XLA Ops:
  0.6 59.8 %shard_map.50 = (f32[1,1024]{1,0:T(1,128)}, f32[1]{0:T(128)}) custom-call(bf16[128,896]{1,0:T(8,128)(2,1)} %bitcast.2, bf16[3584,2560]{1,0:T(8,128)(2,1)} %w_hbm.1, s32[1,128]{1,0:T(1,128)} %bitcast.3), custom_call_target="tpu_custom_call" | custom-call | tf_op jit(solution)/shard_map/pallas_call | solution.py:289
  60.5 1.3 %copy.7 = f32[1,1024]{1,0:T(1,128)} copy(f32[1,1024]{1,0:T(1,128)} %get-tuple-element.4) | data formatting | bytes 8192

commit v3 on v2

--- a/solution.py
+++ b/solution.py
@@ -63,13 +63,13 @@
     pos = {2 * g + c: 2 * i + c for i, g in enumerate(groups) for c in range(2)}
     blocks = n_v * layers
 
-    own = pltpu.make_async_copy(hid_hbm, buf.at[0, pl.ds(0, rows)], own_sem)
+    own = pltpu.make_async_copy(hid_hbm, buf.at[pl.ds(0, rows), pl.ds(0, depth)], own_sem)
     own.start()
     w_copies = []
     for s in range(n_h):
         src = lax.rem(z - s + n_h, n_h)
         copy = pltpu.make_async_copy(
-            w_hbm.at[pl.ds(pl.multiple_of(src * depth, depth), depth)], w.at[s], w_sem.at[s]
+            w_hbm.at[pl.ds(pl.multiple_of(src * depth, depth), depth)], w.at[pl.ds(s * depth, depth)], w_sem.at[s]
         )
         w_copies.append(copy)
 
@@ -91,8 +91,8 @@
     def block_copy(m, s, to_m, to_s, cut, device):
         k = min(len(sends), send_sem.shape[0] - 1)
         return pltpu.make_async_remote_copy(
-            src_ref=buf.at[s, pl.ds(pos[m] * rows + cut * piece, piece)],
-            dst_ref=buf.at[to_s, pl.ds(pos[to_m] * rows + cut * piece, piece)],
+            src_ref=buf.at[pl.ds(pos[m] * rows + cut * piece, piece), pl.ds(s * depth, depth)],
+            dst_ref=buf.at[pl.ds(pos[to_m] * rows + cut * piece, piece), pl.ds(to_s * depth, depth)],
             send_sem=send_sem.at[k],
             recv_sem=recv_sem.at[(to_m * n_h + to_s) * cuts + cut],
             device_id=device, device_id_type=MESH,
@@ -132,6 +132,8 @@
         if s not in waited:
             w_copies[s].wait()
             waited.add(s)
+        k_lo = s * depth // 256 * 256
+        k_hi = (s + 1) * depth // 256 * 256 if s + 1 < n_h else n_h * depth
         lo, size = first * 2 * rows, count * 2 * rows
         step = 1024 if size > 1024 and size % 1024 == 0 else size
 
@@ -140,7 +142,7 @@
             at = pl.ds(pl.multiple_of(n * tile, tile), tile)
             for r in range(lo, lo + size, step):
                 value = jnp.dot(
-                    buf[s, r : r + step, :], w[s, :, at], preferred_element_type=jnp.float32
+                    buf[r : r + step, k_lo:k_hi], w[k_lo:k_hi, at], preferred_element_type=jnp.float32
                 )
                 if s == 0:
                     acc[r : r + step, at] = value
@@ -207,30 +209,33 @@
             else:
                 jobs[t].append((i, 1, s))
 
-    def run(t, lo, hi):
+    def run(t, lo, hi, of=1):
         total = sum(count for _, count, _ in jobs[t]) * tiles
-        begin, end, at = total * lo // 3, total * hi // 3, 0
+        begin, end, at = total * lo // of, total * hi // of, 0
         for first, count, s in jobs[t]:
             first_tile = min(max(0, (begin - at) // count), tiles)
             last_tile = min(max(0, (end - at) // count), tiles)
             multiply(first, count, s, first_tile, last_tile)
             at += count * tiles
 
+    early = min(first for first, _, _ in jobs[last])
+    parts = cuts + 1
     for t in range(last + 1):
         for cut in range(cuts):
             if t > 0:
                 for g, s in events[t]:
                     arrive(g, s, cut)
-            if t > 1 and cut < cuts - 1:
-                run(t - 1, 1, 2)
-        if t > 1:
-            run(t - 1, 1 if cuts == 1 else 2, 3)
-        run(t, 0, 3 if t == 0 or t == last else 1)
-        if t == 1 and last == 1:
-            run(1, 1, 3)
-    for copy in lab_copies:
-        copy.wait()
-    stats(0, len(groups))
+            if t > 1:
+                run(t - 1, cut + 1, cut + 2, parts)
+        if t == last:
+            for copy in lab_copies:
+                copy.wait()
+            stats(0, early)
+        if t in (0, last):
+            run(t, 0, 1)
+        else:
+            run(t, 0, 1, parts)
+    stats(early, len(groups) - early)
 
     for m in range(n_v):
         for l in range(layers):
@@ -295,8 +300,8 @@
         in_specs=[any_space, any_space, vmem],
         out_specs=(vmem, pl.BlockSpec(memory_space=pltpu.SMEM)),
         scratch_shapes=[
-            pltpu.VMEM((n_h, n_v * rows, depth), jnp.bfloat16),
-            pltpu.VMEM((n_h, depth, cols), jnp.bfloat16),
+            pltpu.VMEM((n_v * rows, n_h * depth), jnp.bfloat16),
+            pltpu.VMEM((n_h * depth, cols), jnp.bfloat16),
             pltpu.VMEM((n_v * rows, cols), jnp.float32),
             pltpu.VMEM((n_v, 1, tokens), jnp.int32),
             pltpu.VMEM((3, LANES, LANES), jnp.float32),

time: 63.7 us -> 62.1 us (0.975)
  Pallas kernels: 59.8 us -> 58.2 us
    pallas_call x1, Pallas kernels: 59.8 us -> 58.2 us  [body(): pl.pallas_call(functools.partial(kernel, n_v, n_h, layers), out_shape=(ja...]
where the time goes in v3:
time: 62.1 us; the launch traced here: 61.8 us
  Pallas kernels  58.2 us (94%)
  between operations  2.4 us (4%)
  local copies, waits for them, and re-layouts  1.26 us (2%)
    pallas_call x1, Pallas kernels, body(): pl.pallas_call(functools.partial(kernel, n_v, n_h, layers), out_shape=(ja...  58.2 us
    unnamed x1, local copies, waits for them, and re-layouts  1.26 us

profile of v3, /device:TPU:0, one launch (start us, length us, event | category | flops | bytes accessed | tf_op | source)
XLA Modules:
  0.0 61.8 jit_solution(11997253894053695633)
XLA Ops:
  0.6 58.2 %shard_map.50 = (f32[1,1024]{1,0:T(1,128)}, f32[1]{0:T(128)}) custom-call(bf16[128,896]{1,0:T(8,128)(2,1)} %bitcast.2, bf16[3584,2560]{1,0:T(8,128)(2,1)} %w_hbm.1, s32[1,128]{1,0:T(1,128)} %bitcast.3), custom_call_target="tpu_custom_call" | custom-call | tf_op jit(solution)/shard_map/pallas_call | solution.py:294
  58.8 1.3 %copy.7 = f32[1,1024]{1,0:T(1,128)} copy(f32[1,1024]{1,0:T(1,128)} %get-tuple-element.4) | data formatting | bytes 8192

commit v4 on v3

--- a/solution.py
+++ b/solution.py
@@ -50,7 +50,7 @@
     n_v, n_h, layers,
     hid_hbm, w_hbm, lab_ref,
     loss_ref, mean_ref,
-    buf, w, acc, labs, part, rel_stats, line, plane,
+    buf, w, acc, labs, lanes, rel_stats, line, plane,
     own_sem, w_sem, send_sem, recv_sem, lab_send, lab_recv, line_send, line_recv, plane_send, plane_recv,
 ):
     v, z = lax.axis_index("vocab"), lax.axis_index("hid")
@@ -144,41 +144,49 @@
                 value = jnp.dot(
                     buf[r : r + step, k_lo:k_hi], w[k_lo:k_hi, at], preferred_element_type=jnp.float32
                 )
-                if s == 0:
+                if s > 0:
+                    value = acc[r : r + step, at] + value
+                if s + 1 < n_h:
                     acc[r : r + step, at] = value
-                else:
-                    acc[r : r + step, at] = acc[r : r + step, at] + value
+                    continue
+                here = slice(r, r + step)
+                chunks = [value[:, c : c + LANES] for c in range(0, tile, LANES)]
+                old = lanes[0, here, :]
+                peak = functools.reduce(jnp.maximum, chunks, old)
+                total = lanes[1, here, :] * jnp.exp(old - peak)
+                picked = lanes[2, here, :]
+                wanted = lanes[3, here, :] - (n * tile).astype(jnp.float32)
+                for i, x in enumerate(chunks):
+                    total = total + jnp.exp(x - peak)
+                    picked = picked + jnp.where(wanted == float(i * LANES), x, 0.0)
+                lanes[0, here, :] = peak
+                lanes[1, here, :] = total
+                lanes[2, here, :] = picked
+
+    def prepare():
+        for copy in lab_copies:
+            copy.wait()
+        lane = (lax.broadcasted_iota(jnp.int32, (LANES, LANES), 1) + first_col).astype(jnp.float32)
+
+        @pl.loop(0, blocks)
+        def _(p):
+            at = pl.ds(pl.multiple_of(p * LANES, LANES), LANES)
+            label = jnp.broadcast_to(labs[p // layers].astype(jnp.float32), (LANES, LANES))
+            lanes[0, at, :] = jnp.full((LANES, LANES), -jnp.inf, jnp.float32)
+            lanes[1, at, :] = jnp.zeros((LANES, LANES), jnp.float32)
+            lanes[2, at, :] = jnp.zeros((LANES, LANES), jnp.float32)
+            lanes[3, at, :] = jnp.transpose(label) - lane
 
     def stats(first, count):
-        half = 64
-
         @pl.loop(first * 2 * layers, (first + count) * 2 * layers)
         def _(p):
-            label = labs[p // layers].astype(jnp.float32)
-            label = jnp.transpose(jnp.broadcast_to(label, (LANES, LANES)))
-            lane = lax.broadcasted_iota(jnp.int32, (half, LANES), 1) + first_col
-            lane = lane.astype(jnp.float32)
-            for h in range(LANES // half):
-                at = pl.ds(pl.multiple_of(p * LANES + h * half, half), half)
-                peak = acc[at, 0:LANES]
-                for c in range(LANES, cols, LANES):
-                    peak = jnp.maximum(peak, acc[at, c : c + LANES])
-                here = slice(h * half, (h + 1) * half)
-                part[0, here, :] = peak
-                row_peak = jnp.max(peak, axis=1, keepdims=True)
-                row_peak = jnp.broadcast_to(row_peak, (half, LANES))
-                wanted = label[here] - lane
-                total = jnp.zeros((half, LANES), jnp.float32)
-                picked = jnp.zeros((half, LANES), jnp.float32)
-                for c in range(0, cols, LANES):
-                    x = acc[at, c : c + LANES]
-                    total = total + jnp.exp(x - row_peak)
-                    picked = picked + jnp.where(wanted == float(c), x, 0.0)
-                part[1, here, :] = total
-                part[2, here, :] = picked
-            rel_stats[0, p] = jnp.max(jnp.transpose(part[0]), axis=0, keepdims=True)
-            rel_stats[1, p] = jnp.sum(jnp.transpose(part[1]), axis=0, keepdims=True)
-            rel_stats[2, p] = jnp.sum(jnp.transpose(part[2]), axis=0, keepdims=True)
+            at = pl.ds(pl.multiple_of(p * LANES, LANES), LANES)
+            peak = jnp.transpose(lanes[0, at, :])
+            row_peak = jnp.max(peak, axis=0, keepdims=True)
+            total = jnp.transpose(lanes[1, at, :]) * jnp.exp(peak - row_peak)
+            rel_stats[0, p] = row_peak
+            rel_stats[1, p] = jnp.sum(total, axis=0, keepdims=True)
+            rel_stats[2, p] = jnp.sum(jnp.transpose(lanes[2, at, :]), axis=0, keepdims=True)
 
     for cut in range(cuts):
         arrive(0, 0, cut)
@@ -221,6 +229,8 @@
     early = min(first for first, _, _ in jobs[last])
     parts = cuts + 1
     for t in range(last + 1):
+        if t == min(2, last):
+            prepare()
         for cut in range(cuts):
             if t > 0:
                 for g, s in events[t]:
@@ -228,8 +238,6 @@
             if t > 1:
                 run(t - 1, cut + 1, cut + 2, parts)
         if t == last:
-            for copy in lab_copies:
-                copy.wait()
             stats(0, early)
         if t in (0, last):
             run(t, 0, 1)
@@ -304,7 +312,7 @@
             pltpu.VMEM((n_h * depth, cols), jnp.bfloat16),
             pltpu.VMEM((n_v * rows, cols), jnp.float32),
             pltpu.VMEM((n_v, 1, tokens), jnp.int32),
-            pltpu.VMEM((3, LANES, LANES), jnp.float32),
+            pltpu.VMEM((4, n_v * rows, LANES), jnp.float32),
             pltpu.VMEM((3, blocks, 1, tokens), jnp.float32),
             pltpu.VMEM((n_h, 3 * blocks, tokens), jnp.float32),
             pltpu.VMEM((n_v, 3 * blocks, tokens), jnp.float32),

time: 62.1 us -> 61.5 us (level)
  no operation moved by 1% of the time
where the time goes in v4:
time: 61.5 us; the launch traced here: 61.3 us
  Pallas kernels  57.6 us (94%)
  between operations  2.4 us (4%)
  local copies, waits for them, and re-layouts  1.26 us (2%)
    pallas_call x1, Pallas kernels, body(): pl.pallas_call(functools.partial(kernel, n_v, n_h, layers), out_shape=(ja...  57.6 us
    unnamed x1, local copies, waits for them, and re-layouts  1.26 us

profile of v4, /device:TPU:0, one launch (start us, length us, event | category | flops | bytes accessed | tf_op | source)
XLA Modules:
  0.0 61.3 jit_solution(13578928965915438067)
XLA Ops:
  0.6 57.6 %shard_map.50 = (f32[1,1024]{1,0:T(1,128)}, f32[1]{0:T(128)}) custom-call(bf16[128,896]{1,0:T(8,128)(2,1)} %bitcast.2, bf16[3584,2560]{1,0:T(8,128)(2,1)} %w_hbm.1, s32[1,128]{1,0:T(1,128)} %bitcast.3), custom_call_target="tpu_custom_call" | custom-call | tf_op jit(solution)/shard_map/pallas_call | solution.py:302
  58.3 1.3 %copy.7 = f32[1,1024]{1,0:T(1,128)} copy(f32[1,1024]{1,0:T(1,128)} %get-tuple-element.4) | data formatting | bytes 8192
